TPU v7x, 512 devices: a whole 4x4x16 slice. The times are simulated.
512 devices in a mesh: section: 2 (over y_hi), wide: 64 (over z, y_lo, core), narrow: 4 (over x).
Axes of the slice: x: 4, y: 4 (y_hi: 2, y_lo: 2; y = y_hi * 2 + y_lo), z: 16, core: 2. Of those that a mesh axis runs over, the one named last changes fastest.
Arguments:
- token_shard: int32 [16384, 1], P(('section', 'wide')), may hold values from 0 to 127; in each aligned block of 128 rows (0 to 127, 128 to 255, ...) at most 2 rows name the same one
- token_row: int32 [16384], P(('section', 'wide')), may hold values from 0 to 511
- table: bfloat16 [65536, 8192], P(('section', 'wide'), 'narrow'), may hold values from -51 to 51
- gain: float32 [8192], P('narrow'), may hold values from 0.1 to 1.9
- key_value_weight: bfloat16 [2048, 8192], P(('section', 'wide'), 'narrow'), may hold values from -0.0625 to 0.0625
- kv_target: bfloat16 [16384, 2048], P(('section', 'wide'), 'narrow'), may hold values from -6 to 6
Outputs:
- table_grad: bfloat16 [65536, 8192], P(('section', 'wide'), 'narrow')
Inputs may be any that keep to these rules, and one draw needn't show every extreme that they name: `token_shard`: among the rows of one device, no value is named by more than 2 rows.
All inputs are finite; a program needn't handle non-finite values.
Results may differ from a plain program's by a relative error of at most 0.0056.
Values may be sent and summed in bfloat16 or wider, within the bound.
A program may use at most 64 MiB of HBM per device.

v0:
```python
import jax
import jax.numpy as jnp
from jax import lax
from jax.sharding import PartitionSpec as P

D = 8192
EPSILON = 1e-05


def contract_last(left, right):
    return lax.dot_general(
        left, right, (((1,), (1,)), ((), ())), preferred_element_type=jnp.float32
    )


def on_device(token_shard, token_row, table, gain, key_value_weight, kv_target):
    tokens_here = token_row.shape[0]
    owners = lax.axis_size(("section", "wide"))
    slot_count = 2 * tokens_here // owners
    width_here = table.shape[1]
    shard_of = token_shard[:, 0]
    membership = (shard_of[:, None] == jnp.arange(owners, dtype=jnp.int32)[None, :]).astype(
        jnp.int32
    )
    ranking = jnp.sum((jnp.cumsum(membership, axis=0) - 1) * membership, axis=1)
    position = shard_of * slot_count + ranking
    requests = (
        jnp.full((owners * slot_count,), -1, jnp.int32)
        .at[position]
        .set(token_row)
        .reshape(owners, slot_count)
    )
    holder = (
        jnp.full((owners * slot_count,), -1, jnp.int32)
        .at[position]
        .set(jnp.arange(tokens_here, dtype=jnp.int32))
    )
    wanted = lax.all_to_all(requests, ("section", "wide"), split_axis=0, concat_axis=0, tiled=True)
    present = wanted >= 0
    picked = jnp.take(table, jnp.where(present, wanted, 0), axis=0)
    returned = lax.all_to_all(
        jnp.where(present[..., None], picked, jnp.zeros((), table.dtype)),
        ("section", "wide"),
        split_axis=0,
        concat_axis=0,
        tiled=True,
    )
    hidden = jnp.take(returned.reshape(owners * slot_count, width_here), position, axis=0)
    rows_float = hidden.astype(jnp.float32)
    mean_square = lax.psum(jnp.sum(rows_float * rows_float, axis=1), "narrow") / D
    row_scale = lax.rsqrt(mean_square + EPSILON)
    normed = (rows_float * row_scale[:, None] * gain[None, :]).astype(jnp.bfloat16)
    weight_full = lax.all_gather(key_value_weight, ("section", "wide"), axis=0, tiled=True)
    partial_value = contract_last(normed, weight_full)
    projected = lax.psum_scatter(partial_value, "narrow", scatter_dimension=1, tiled=True)
    residual = (projected - kv_target.astype(jnp.float32)).astype(jnp.bfloat16)
    residual_full = lax.all_gather(residual, "narrow", axis=1, tiled=True)
    back_rows = jnp.dot(residual_full, weight_full, preferred_element_type=jnp.float32)
    weighted = back_rows * gain[None, :]
    inner_sum = lax.psum(jnp.sum(weighted * rows_float, axis=1), "narrow")
    grad_rows = (
        row_scale[:, None] * weighted - rows_float * (row_scale**3 * inner_sum / D)[:, None]
    ).astype(jnp.bfloat16)
    occupied = holder >= 0
    outgoing = jnp.where(
        occupied[:, None],
        jnp.take(grad_rows, jnp.where(occupied, holder, 0), axis=0),
        jnp.zeros((), jnp.bfloat16),
    )
    incoming = lax.all_to_all(
        outgoing.reshape(owners, slot_count, width_here),
        ("section", "wide"),
        split_axis=0,
        concat_axis=0,
        tiled=True,
    )
    vocab_rows = table.shape[0]
    matches = (
        wanted.reshape(1, owners * slot_count) == jnp.arange(vocab_rows, dtype=jnp.int32)[:, None]
    ).astype(jnp.bfloat16)
    table_grad = jnp.dot(
        matches,
        incoming.reshape(owners * slot_count, width_here),
        preferred_element_type=jnp.float32,
    )
    return table_grad.astype(jnp.bfloat16)


def solution(mesh):
    return jax.shard_map(
        on_device,
        mesh=mesh,
        in_specs=(
            P(("section", "wide"), None),
            P(("section", "wide")),
            P(("section", "wide"), "narrow"),
            P("narrow"),
            P(("section", "wide"), "narrow"),
            P(("section", "wide"), "narrow"),
        ),
        out_specs=P(("section", "wide"), "narrow"),
        check_vma=False,
    )
```

profile of v0, /device:TPU:1, one launch (start us, length us, event | category | flops | bytes accessed | tf_op | source)
XLA Modules:
  0.0 417.6 jit_solution(1082262638751350529)
XLA Ops:
  6.5 0.0 copy-start
  6.5 0.0 all-gather.2.cloned.1.call-start
  6.5 0.7 all-gather.2.cloned.1.call-update
  7.3 0.7 fusion.11
  8.0 0.2 reduce_window_sum.11
  8.2 0.8 select_reduce_fusion
  9.0 0.7 and_bitcast_fusion
  9.7 1.1 scatter_custom_fusion
  10.8 0.1 all_to_all.16
  10.9 35.0 %all_to_all.25 = s32[128,1,2]{2,1,0:T(1,128)S(1)} all-to-all(s32[128,1,2]{2,1,0:T(1,128)S(1)} %bitcast.20), channel_id=1, replica_groups=mesh['section'=2,'wide'=64,'narrow'=4] {'section','wide'}, dimensions={0} | all-to-all | bytes 2048 | tf_op jit(solution)/shard_map/all_to_all | solution.py:38
  45.9 0.1 reshape.81
  46.1 0.0 copy-done
  46.1 1.4 gather_fusion
  47.5 0.0 copy-start.3
  47.5 1.5 reshape.80
  49.0 3.2 broadcast_select_fusion.1
  52.3 7.8 %all-to-all-start.1 = ((bf16[128,2,2048]{2,1,0:T(2,128)(2,1)}), bf16[128,2,2048]{2,1,0:T(2,128)(2,1)}, u32[]{:S(2)}, u32[]{:S(2)}) async-start(bf16[128,2,2048]{2,1,0:T(2,128)(2,1)} %broadcast_select_fusion.1), calls=%async_computation.1 | async-start | bytes 2097152 | tf_op jit(solution)/shard_map/all_to_all | solution.py:41
  60.1 0.0 reduce-scatter.2.cloned.1.call-start
  60.2 58.5 %all-to-all-done.1 = bf16[128,2,2048]{2,1,0:T(2,128)(2,1)} async-done(((bf16[128,2,2048]{2,1,0:T(2,128)(2,1)}), bf16[128,2,2048]{2,1,0:T(2,128)(2,1)}, u32[]{:S(2)}, u32[]{:S(2)}) %all-to-all-start.1) | async-done | bytes 1048608 | tf_op jit(solution)/shard_map/all_to_all | solution.py:41
  118.7 1.5 reshape.77
  120.1 0.0 copy-start.2
  120.2 1.8 gather_fusion.1
  121.9 0.0 copy-start.1
  121.9 1.4 fusion
  123.3 8.5 %psum.14 = f32[128]{0:T(128)S(1)} all-reduce(f32[128]{0:T(128)S(1)} %fusion), channel_id=1, replica_groups=mesh['section'=2,'wide'=64,'narrow'=4] {'narrow'}, use_global_device_ids=true, to_apply=%region_5.6 | all-reduce | flops 128 | bytes 1024 | tf_op jit(solution)/shard_map/psum | solution.py:50
  131.8 129.1 %all-gather.2.cloned.1.call-done = bf16[2048,2048]{1,0:T(8,128)(2,1)} async-done(((bf16[16,2048]{1,0:T(8,128)(2,1)}), bf16[2048,2048]{1,0:T(8,128)(2,1)}) %all-gather.2.cloned.1.call-update) | async-done | bytes 8388624 | tf_op jit(solution)/shard_map/all_gather | solution.py:53
  260.9 0.0 copy-done.3
  260.9 7.4 %fusion.6 = f32[128,2048]{1,0:T(8,128)} fusion(bf16[2048,2048]{1,0:T(8,128)(2,1)} %all-gather.2.cloned.1.call-done, f32[2048]{0:T(1024)S(1)} %copy-done.3, f32[128]{0:T(128)S(1)} %add_rsqrt_fusion, bf16[128,2048]{1,0:T(8,128)(2,1)} %gather_fusion.1, pred[128]{0:T(512)(128)(4,1)S(1)} %get-tuple-element.7), kind=kOutput, calls=%fused_computation.21 | convolution fusion | flops 1075052544 | bytes 9970304 | tf_op jit(solution)/shard_map/dot_general | solution.py:11
  268.4 0.0 reduce-scatter.2.cloned.1.call-update
  268.4 1.0 scatter_custom_fusion.1
  269.4 0.2 broadcast_in_dim.71
  269.6 0.2 broadcast_in_dim.73
  269.7 26.5 %reduce-scatter.2.cloned.1.call-done = f32[128,512]{1,0:T(8,128)} async-done(((f32[128,2048]{1,0:T(8,128)}), f32[128,512]{1,0:T(8,128)}) %reduce-scatter.2.cloned.1.call-update) | async-done | bytes 262160 | tf_op jit(solution)/shard_map/reduce_scatter | solution.py:55
  296.3 0.0 copy-done.2
  296.3 1.0 subtract_convert_fusion
  297.3 10.7 %all_gather.7 = bf16[128,2048]{1,0:T(8,128)(2,1)S(1)} all-gather(bf16[128,512]{1,0:T(8,128)(2,1)S(1)} %subtract_convert_fusion), channel_id=1, replica_groups=mesh['section'=2,'wide'=64,'narrow'=4] {'narrow'}, dimensions={1}, use_global_device_ids=true | all-gather | bytes 655360 | tf_op jit(solution)/shard_map/all_gather | solution.py:57
  307.9 0.0 copy-done.1
  307.9 5.7 %fusion.3 = (f32[128]{0:T(128)S(1)}, f32[128,2048]{1,0:T(8,128)}) fusion(bf16[128,2048]{1,0:T(8,128)(2,1)S(1)} %copy-done.1, pred[128]{0:T(512)(128)(4,1)S(1)} %get-tuple-element.7, f32[2048]{0:T(1024)S(1)} %copy-done.3, bf16[128,2048]{1,0:T(8,128)(2,1)S(1)} %all_gather.7, bf16[2048,2048]{1,0:T(8,128)(2,1)} %all-gather.2.cloned.1.call-done), kind=kOutput, calls=%fused_computation.18 | convolution fusion | flops 1075052416 | bytes 10494592 | tf_op jit(solution)/shard_map/dot_general | solution.py:58
  313.7 6.0 %psum.15 = f32[128]{0:T(128)S(1)} all-reduce(f32[128]{0:T(128)S(1)} %get-tuple-element.12), channel_id=1, replica_groups=mesh['section'=2,'wide'=64,'narrow'=4] {'narrow'}, use_global_device_ids=true, to_apply=%region_8.9 | all-reduce | flops 128 | bytes 1024 | tf_op jit(solution)/shard_map/psum | solution.py:60
  319.7 1.5 fusion.5
  321.2 2.3 gather_fusion.2
  323.5 1.7 gather.17
  325.3 2.4 broadcast_select_fusion.3
  327.7 23.3 %all-to-all-start.2 = ((bf16[128,2,2048]{2,1,0:T(2,128)(2,1)}), bf16[128,2,2048]{2,1,0:T(2,128)(2,1)S(1)}, u32[]{:S(2)}, u32[]{:S(2)}) async-start(bf16[128,2,2048]{2,1,0:T(2,128)(2,1)} %broadcast_select_fusion.3), calls=%async_computation.3 | async-start | bytes 2097152 | tf_op jit(solution)/shard_map/all_to_all | solution.py:70
  351.0 0.6 broadcast.120
  351.5 0.8 reduce.3
  352.4 0.1 eq.34
  352.5 53.7 %all-to-all-done.2 = bf16[128,2,2048]{2,1,0:T(2,128)(2,1)S(1)} async-done(((bf16[128,2,2048]{2,1,0:T(2,128)(2,1)}), bf16[128,2,2048]{2,1,0:T(2,128)(2,1)S(1)}, u32[]{:S(2)}, u32[]{:S(2)}) %all-to-all-start.2) | async-done | bytes 1048608 | tf_op jit(solution)/shard_map/all_to_all | solution.py:70
  406.3 1.2 reshape.78
  407.5 3.3 convolution_convert_fusion
  (9 shorter events, 0.1 us)
Async XLA Ops:
  6.5 39.6 %copy-start = (bf16[512,2048]{1,0:T(8,128)(2,1)S(1)}, bf16[512,2048]{1,0:T(8,128)(2,1)}, u32[]{:S(2)}) copy-start(bf16[512,2048]{1,0:T(8,128)(2,1)} %param.8) | copy-start | bytes 6291460
  6.5 254.4 %all-gather.2.cloned.1.call-start = ((), (), s32[]{:S(2)}) async-start(), calls=%async_computation.4 | async-start | bytes 8454144 | tf_op jit(solution)/shard_map/all_gather | solution.py:53
  47.5 213.5 %copy-start.3 = (f32[2048]{0:T(1024)S(1)}, f32[2048]{0:T(1024)}, u32[]{:S(2)}) copy-start(f32[2048]{0:T(1024)} %param.9) | copy-start | bytes 24580
  52.3 66.4 %all-to-all-start.1 = ((bf16[128,2,2048]{2,1,0:T(2,128)(2,1)}), bf16[128,2,2048]{2,1,0:T(2,128)(2,1)}, u32[]{:S(2)}, u32[]{:S(2)}) async-start(bf16[128,2,2048]{2,1,0:T(2,128)(2,1)} %broadcast_select_fusion.1), calls=%async_computation.1 | async-start | bytes 2097152 | tf_op jit(solution)/shard_map/all_to_all | solution.py:41
  60.1 236.1 %reduce-scatter.2.cloned.1.call-start = ((), (), s32[]{:S(2)}) async-start(), calls=%async_computation.5 | async-start | bytes 1310720 | tf_op jit(solution)/shard_map/reduce_scatter | solution.py:55
  120.1 176.1 %copy-start.2 = (bf16[128,512]{1,0:T(8,128)(2,1)S(1)}, bf16[128,512]{1,0:T(8,128)(2,1)}, u32[]{:S(2)}) copy-start(bf16[128,512]{1,0:T(8,128)(2,1)} %param.11) | copy-start | bytes 393220
  121.9 186.0 %copy-start.1 = (bf16[128,2048]{1,0:T(8,128)(2,1)S(1)}, bf16[128,2048]{1,0:T(8,128)(2,1)}, u32[]{:S(2)}) copy-start(bf16[128,2048]{1,0:T(8,128)(2,1)} %gather_fusion.1) | copy-start | bytes 1572868
  327.7 78.6 %all-to-all-start.2 = ((bf16[128,2,2048]{2,1,0:T(2,128)(2,1)}), bf16[128,2,2048]{2,1,0:T(2,128)(2,1)S(1)}, u32[]{:S(2)}, u32[]{:S(2)}) async-start(bf16[128,2,2048]{2,1,0:T(2,128)(2,1)} %broadcast_select_fusion.3), calls=%async_computation.3 | async-start | bytes 2097152 | tf_op jit(solution)/shard_map/all_to_all | solution.py:70
Sparse Core Ops, SparseCore 0:
  9.5 251.3 all-gather.1
  268.5 27.6 reduce-scatter.1
where the time goes:
time: 418 us
  waiting for transfers between devices  269 us (64%)
  blocking collectives  60.2 us (14%)
  starting transfers between devices  31.1 us (7%)
  matrix products  16.4 us (4%)
  local copies, waits for them, and re-layouts  14.8 us (4%)
  between operations  13.6 us (3%)
  other arithmetic  12.9 us (3%)
    all_gather x1, waiting for transfers between devices, on_device(): lax.all_gather(key_value_weight, ('section', 'wide'), axis=0, tiled=True)  129 us
    all_to_all x1, waiting for transfers between devices, on_device(): lax.all_to_all(jnp.where(present[..., None], picked, jnp.zeros((), table....  58.5 us
    all_to_all x1, waiting for transfers between devices, on_device(): lax.all_to_all(outgoing.reshape(owners, slot_count, width_here), ('sectio...  53.7 us
    all_to_all x1, blocking collectives, on_device(): lax.all_to_all(requests, ('section', 'wide'), split_axis=0, concat_axis=0...  35 us
    reduce_scatter x1, waiting for transfers between devices, on_device(): lax.psum_scatter(partial_value, 'narrow', scatter_dimension=1, tiled=True)  26.5 us
    all_to_all x1, starting transfers between devices, on_device(): lax.all_to_all(outgoing.reshape(owners, slot_count, width_here), ('sectio...  23.3 us
    all_gather x1, blocking collectives, on_device(): residual_full = lax.all_gather(residual, 'narrow', axis=1, tiled=True)  10.7 us
    psum x1, blocking collectives, on_device(): lax.psum(jnp.sum(rows_float * rows_float, axis=1), 'narrow') / D  8.48 us
  transfers between devices with their start and end apart: 4, of which 4 were waited for; matrix products, arithmetic and copies ran while one was open for 4% of the time, Pallas kernels for 0%

commit v1 on v0

--- a/solution.py
+++ b/solution.py
@@ -5,6 +5,15 @@
 
 D = 8192
 EPSILON = 1e-05
+
+
+def time_copies_by_axis(point, array_axis):
+    return jnp.concatenate(
+        lax.all_to_all(
+            jnp.stack([point] * lax.axis_size(("section", "wide"))), ("section", "wide"), 0, 0
+        ),
+        axis=array_axis,
+    )
 
 
 def contract_last(left, right):
@@ -50,7 +59,7 @@
     mean_square = lax.psum(jnp.sum(rows_float * rows_float, axis=1), "narrow") / D
     row_scale = lax.rsqrt(mean_square + EPSILON)
     normed = (rows_float * row_scale[:, None] * gain[None, :]).astype(jnp.bfloat16)
-    weight_full = lax.all_gather(key_value_weight, ("section", "wide"), axis=0, tiled=True)
+    weight_full = time_copies_by_axis(key_value_weight, 0)
     partial_value = contract_last(normed, weight_full)
     projected = lax.psum_scatter(partial_value, "narrow", scatter_dimension=1, tiled=True)
     residual = (projected - kv_target.astype(jnp.float32)).astype(jnp.bfloat16)

time: 418 us -> 645 us (1.54)
  waiting for transfers between devices: 269 us -> 429 us
  blocking collectives: 60.2 us -> 123 us
    all_to_all x1, waiting for transfers between devices: 58.5 us -> 351 us  [time_copies_by_axis(): lax.all_to_all(jnp.stack([point] * lax.axis_size(('section', 'wide'))), (...]
    all_gather x1 -> x0, waiting for transfers between devices: 129 us -> none  [on_device(): lax.all_gather(key_value_weight, ('section', 'wide'), axis=0, tiled=True)]
    all_to_all x0 -> x1, blocking collectives: none -> 61.6 us  [on_device(): lax.all_to_all(jnp.where(present[..., None], picked, jnp.zeros((), table....]
  transfers between devices with their start and end apart: 4 -> 3, of which waited for: 4 -> 3; matrix products, arithmetic and copies ran while one was open for 4% -> 1% of each run, Pallas kernels for 0% -> 0%
where the time goes in v1:
time: 645 us
  waiting for transfers between devices  429 us (67%)
  blocking collectives  123 us (19%)
  starting transfers between devices  31.3 us (5%)
  local copies, waits for them, and re-layouts  19 us (3%)
  matrix products  16.4 us (3%)
  between operations  13.6 us (2%)
  other arithmetic  12.2 us (2%)
    all_to_all x1, waiting for transfers between devices, time_copies_by_axis(): lax.all_to_all(jnp.stack([point] * lax.axis_size(('section', 'wide'))), (...  351 us
    all_to_all x1, blocking collectives, on_device(): lax.all_to_all(jnp.where(present[..., None], picked, jnp.zeros((), table....  61.6 us
    all_to_all x1, waiting for transfers between devices, on_device(): lax.all_to_all(outgoing.reshape(owners, slot_count, width_here), ('sectio...  53.7 us
    all_to_all x1, blocking collectives, on_device(): lax.all_to_all(requests, ('section', 'wide'), split_axis=0, concat_axis=0...  35 us
    reduce_scatter x1, waiting for transfers between devices, on_device(): lax.psum_scatter(partial_value, 'narrow', scatter_dimension=1, tiled=True)  24.6 us
    all_to_all x1, starting transfers between devices, on_device(): lax.all_to_all(outgoing.reshape(owners, slot_count, width_here), ('sectio...  23.3 us
  transfers between devices with their start and end apart: 3, of which 3 were waited for; matrix products, arithmetic and copies ran while one was open for 1% of the time, Pallas kernels for 0%

profile of v1, /device:TPU:1, one launch (start us, length us, event | category | flops | bytes accessed | tf_op | source)
XLA Modules:
  0.0 644.7 jit_solution(306322877704074395)
XLA Ops:
  6.5 0.0 copy-start
  6.5 0.0 copy-start.3
  6.5 0.9 fusion.11
  7.4 0.2 reduce_window_sum.11
  7.6 0.8 select_reduce_fusion
  8.4 0.7 and_bitcast_fusion
  9.1 1.1 scatter_custom_fusion
  10.2 0.1 all_to_all.19
  10.4 35.0 %all_to_all.30 = s32[128,1,2]{2,1,0:T(1,128)S(1)} all-to-all(s32[128,1,2]{2,1,0:T(1,128)S(1)} %bitcast.23), channel_id=1, replica_groups=mesh['section'=2,'wide'=64,'narrow'=4] {'section','wide'}, dimensions={0} | all-to-all | bytes 2048 | tf_op jit(solution)/shard_map/all_to_all | solution.py:47
  45.4 0.1 reshape.87
  45.6 0.0 copy-done
  45.6 1.4 gather_fusion
  46.9 1.5 reshape.86
  48.4 2.5 broadcast_select_fusion.1
  50.9 61.6 %all_to_all.31 = bf16[128,2,2048]{2,1,0:T(2,128)(2,1)} all-to-all(bf16[128,2,2048]{2,1,0:T(2,128)(2,1)S(1)} %broadcast_select_fusion.1), channel_id=1, replica_groups=mesh['section'=2,'wide'=64,'narrow'=4] {'section','wide'}, dimensions={0} | all-to-all | bytes 2097152 | tf_op jit(solution)/shard_map/all_to_all | solution.py:50
  112.5 0.0 copy-done.3
  112.5 4.3 stack.2
  116.8 0.0 copy-start.4
  116.8 8.0 %all-to-all-start.2 = ((bf16[128,16,2048]{2,1,0:T(8,128)(2,1)}), bf16[128,16,2048]{2,1,0:T(8,128)(2,1)}, u32[]{:S(2)}, u32[]{:S(2)}) async-start(bf16[128,16,2048]{2,1,0:T(8,128)(2,1)} %stack.2), calls=%async_computation.2 | async-start | bytes 16777216 | tf_op jit(solution)/shard_map/all_to_all | solution.py:12
  124.8 0.0 reduce-scatter.2.cloned.1.call-start
  124.8 1.5 reshape.82
  126.3 0.0 copy-start.2
  126.3 1.7 gather_fusion.1
  128.1 0.0 copy-start.1
  128.1 1.4 fusion
  129.5 9.4 %psum.14 = f32[128]{0:T(128)S(1)} all-reduce(f32[128]{0:T(128)S(1)} %fusion), channel_id=1, replica_groups=mesh['section'=2,'wide'=64,'narrow'=4] {'narrow'}, use_global_device_ids=true, to_apply=%region_5.6 | all-reduce | flops 128 | bytes 1024 | tf_op jit(solution)/shard_map/psum | solution.py:59
  138.9 351.1 %all-to-all-done.2 = bf16[128,16,2048]{2,1,0:T(8,128)(2,1)} async-done(((bf16[128,16,2048]{2,1,0:T(8,128)(2,1)}), bf16[128,16,2048]{2,1,0:T(8,128)(2,1)}, u32[]{:S(2)}, u32[]{:S(2)}) %all-to-all-start.2) | async-done | bytes 8388640 | tf_op jit(solution)/shard_map/all_to_all | solution.py:12
  490.0 0.0 copy-done.4
  490.0 7.4 %fusion.6 = f32[128,2048]{1,0:T(8,128)} fusion(bf16[2048,2048]{1,0:T(8,128)(2,1)} %bitcast.7, f32[2048]{0:T(1024)S(1)} %copy-done.4, f32[128]{0:T(128)S(1)} %add_rsqrt_fusion, bf16[128,2048]{1,0:T(8,128)(2,1)} %gather_fusion.1, pred[128]{0:T(512)(128)(4,1)S(1)} %get-tuple-element.7), kind=kOutput, calls=%fused_computation.21 | convolution fusion | flops 1075052544 | bytes 9970304 | tf_op jit(solution)/shard_map/dot_general | solution.py:20
  497.4 0.0 reduce-scatter.2.cloned.1.call-update
  497.5 1.0 scatter_custom_fusion.1
  498.5 0.2 broadcast_in_dim.73
  498.6 0.2 broadcast_in_dim.71
  498.8 24.6 %reduce-scatter.2.cloned.1.call-done = f32[128,512]{1,0:T(8,128)} async-done(((f32[128,2048]{1,0:T(8,128)}), f32[128,512]{1,0:T(8,128)}) %reduce-scatter.2.cloned.1.call-update) | async-done | bytes 262160 | tf_op jit(solution)/shard_map/reduce_scatter | solution.py:64
  523.4 0.0 copy-done.2
  523.4 1.0 subtract_convert_fusion
  524.4 10.7 %all_gather.3 = bf16[128,2048]{1,0:T(8,128)(2,1)S(1)} all-gather(bf16[128,512]{1,0:T(8,128)(2,1)S(1)} %subtract_convert_fusion), channel_id=1, replica_groups=mesh['section'=2,'wide'=64,'narrow'=4] {'narrow'}, dimensions={1}, use_global_device_ids=true | all-gather | bytes 655360 | tf_op jit(solution)/shard_map/all_gather | solution.py:66
  535.1 0.0 copy-done.1
  535.1 5.7 fusion.3
  540.8 6.0 psum.15
  546.8 1.5 fusion.5
  548.3 2.3 gather_fusion.2
  550.6 1.7 gather.17
  552.4 2.4 broadcast_select_fusion.3
  554.8 23.3 %all-to-all-start.3 = ((bf16[128,2,2048]{2,1,0:T(2,128)(2,1)}), bf16[128,2,2048]{2,1,0:T(2,128)(2,1)S(1)}, u32[]{:S(2)}, u32[]{:S(2)}) async-start(bf16[128,2,2048]{2,1,0:T(2,128)(2,1)} %broadcast_select_fusion.3), calls=%async_computation.4 | async-start | bytes 2097152 | tf_op jit(solution)/shard_map/all_to_all | solution.py:79
  578.1 0.6 broadcast.122
  578.7 0.8 reduce.3
  579.6 0.1 eq.34
  579.7 53.7 %all-to-all-done.3 = bf16[128,2,2048]{2,1,0:T(2,128)(2,1)S(1)} async-done(((bf16[128,2,2048]{2,1,0:T(2,128)(2,1)}), bf16[128,2,2048]{2,1,0:T(2,128)(2,1)S(1)}, u32[]{:S(2)}, u32[]{:S(2)}) %all-to-all-start.3) | async-done | bytes 1048608 | tf_op jit(solution)/shard_map/all_to_all | solution.py:79
  633.4 1.2 reshape.84
  634.6 3.3 convolution_convert_fusion
  (9 shorter events, 0.1 us)
Async XLA Ops:
  6.5 39.0 %copy-start = (bf16[512,2048]{1,0:T(8,128)(2,1)S(1)}, bf16[512,2048]{1,0:T(8,128)(2,1)}, u32[]{:S(2)}) copy-start(bf16[512,2048]{1,0:T(8,128)(2,1)} %param.8) | copy-start | bytes 6291460
  6.5 106.0 %copy-start.3 = (bf16[16,2048]{1,0:T(8,128)(2,1)S(1)}, bf16[16,2048]{1,0:T(8,128)(2,1)}, u32[]{:S(2)}) copy-start(bf16[16,2048]{1,0:T(8,128)(2,1)} %param.10) | copy-start | bytes 196612
  116.8 373.2 %copy-start.4 = (f32[2048]{0:T(1024)S(1)}, f32[2048]{0:T(1024)}, u32[]{:S(2)}) copy-start(f32[2048]{0:T(1024)} %param.9) | copy-start | bytes 24580
  116.8 373.2 %all-to-all-start.2 = ((bf16[128,16,2048]{2,1,0:T(8,128)(2,1)}), bf16[128,16,2048]{2,1,0:T(8,128)(2,1)}, u32[]{:S(2)}, u32[]{:S(2)}) async-start(bf16[128,16,2048]{2,1,0:T(8,128)(2,1)} %stack.2), calls=%async_computation.2 | async-start | bytes 16777216 | tf_op jit(solution)/shard_map/all_to_all | solution.py:12
  124.8 398.6 %reduce-scatter.2.cloned.1.call-start = ((), (), s32[]{:S(2)}) async-start(), calls=%async_computation.5 | async-start | bytes 1310720 | tf_op jit(solution)/shard_map/reduce_scatter | solution.py:64
  126.3 397.1 %copy-start.2 = (bf16[128,512]{1,0:T(8,128)(2,1)S(1)}, bf16[128,512]{1,0:T(8,128)(2,1)}, u32[]{:S(2)}) copy-start(bf16[128,512]{1,0:T(8,128)(2,1)} %param.11) | copy-start | bytes 393220
  128.1 407.0 %copy-start.1 = (bf16[128,2048]{1,0:T(8,128)(2,1)S(1)}, bf16[128,2048]{1,0:T(8,128)(2,1)}, u32[]{:S(2)}) copy-start(bf16[128,2048]{1,0:T(8,128)(2,1)} %gather_fusion.1) | copy-start | bytes 1572868
  554.8 78.6 %all-to-all-start.3 = ((bf16[128,2,2048]{2,1,0:T(2,128)(2,1)}), bf16[128,2,2048]{2,1,0:T(2,128)(2,1)S(1)}, u32[]{:S(2)}, u32[]{:S(2)}) async-start(bf16[128,2,2048]{2,1,0:T(2,128)(2,1)} %broadcast_select_fusion.3), calls=%async_computation.4 | async-start | bytes 2097152 | tf_op jit(solution)/shard_map/all_to_all | solution.py:79
Sparse Core Ops, SparseCore 0:
  497.6 25.7 reduce-scatter.1
